TPU v7x, 32 devices: a whole 2x2x4 slice. The times are simulated.
32 devices in a mesh: dp: 8 (over z, x), mp: 4 (over y, core).
Axes of the slice: x: 2, y: 2, z: 4, core: 2. Of those that a mesh axis runs over, the one named last changes fastest.
Arguments:
- rows: float32 [16384, 1280], P(('dp', 'mp')), may hold values from -6 to 6
- lengths: int32 [256], P('dp'), may hold values from 1 to 64, as said below
- freq_class: int32 [256], P(('dp', 'mp')), may hold values from 0 to 2
- freq_table: float32 [3, 1280], replicated, may hold values from -3 to 3
- gain_attn: float32 [1280], replicated, may hold values from 0.5 to 1.5
- gain_mlp: float32 [1280], replicated, may hold values from 0.5 to 1.5
- w_qkv: float32 [3, 1280, 1280], P(None, None, 'mp'), may hold values from -0.15625 to 0.15625
- w_out: float32 [1280, 1280], P('mp'), may hold values from -0.5 to 0.5
- w_gate_up: float32 [2, 1280, 5120], P(None, None, 'mp'), may hold values from -0.15625 to 0.15625
- w_down: float32 [5120, 1280], P('mp'), may hold values from -0.15625 to 0.15625
- cotangent: float32 [16384, 1280], P(('dp', 'mp')), may hold values from -6 to 6
Outputs:
- output: float32 [16384, 1280], P(('dp', 'mp'))
- grad_rows: float32 [16384, 1280], P(('dp', 'mp'))
- grad_qkv: float32 [3, 1280, 1280], P(None, None, 'mp')
- grad_out: float32 [1280, 1280], P('mp')
- grad_gate_up: float32 [2, 1280, 5120], P(None, None, 'mp')
- grad_down: float32 [5120, 1280], P('mp')
- grad_gain_attn: float32 [1280], replicated
- grad_gain_mlp: float32 [1280], replicated
- grad_table: float32 [3, 1280], replicated
Inputs may be any that keep to these rules, and one draw needn't show every extreme that they name: `lengths`: the valid patches of a series are the last of its 64 slots; some series has all 64, and some only one.
All inputs are finite; a program needn't handle non-finite values.
Results may differ from a plain program's by a relative error of at most 0.02.
Values may be sent and summed in bfloat16 or wider, within the bound.
A program may use at most 256 MiB of HBM per device.

v0:
```python
import jax
import jax.numpy as jnp
from jax import lax
from jax.sharding import PartitionSpec as P

HS = 80
NFREQ = 3
SEQ = 64
EPSILON = 1e-06
NEGATIVE = -1e30
HIGHEST = lax.Precision.HIGHEST


def rotate(values, cosines, sines):
    half_width = values.shape[-1] // 2
    first_half = values[..., :half_width]
    second_half = values[..., half_width:]
    return jnp.concatenate(
        [first_half * cosines - second_half * sines, second_half * cosines + first_half * sines], -1
    )


def series_tables(series_lengths):
    places = jnp.arange(SEQ, dtype=jnp.int32)
    starts = SEQ - series_lengths
    valid_mask = places[None, :] >= starts[:, None]
    positions = (places[None, :] - starts[:, None]).astype(jnp.float32)
    frequency = 10000.0 ** (-2.0 * jnp.arange(HS // 2, dtype=jnp.float32) / HS)
    angles = positions[:, :, None] * frequency[None, None, :]
    return (valid_mask, jnp.cos(angles)[:, :, None, :], jnp.sin(angles)[:, :, None, :])


def allowed_pairs(valid_mask):
    places = jnp.arange(SEQ, dtype=jnp.int32)
    causal = places[:, None] >= places[None, :]
    itself = places[:, None] == places[None, :]
    return causal[None, None] & (valid_mask[:, None, None, :] | itself[None, None])


def norm_forward(values, gain):
    inverse = lax.rsqrt(jnp.mean(values * values, -1, keepdims=True) + EPSILON)
    return ((values * inverse * gain).astype(jnp.bfloat16), inverse)


def norm_backward(values, inverse, gain, grad_normed):
    normal = values * inverse
    grad_gain = jnp.sum(grad_normed * normal, 0)
    scaled = grad_normed * gain
    grad_values = inverse * (scaled - normal * jnp.mean(scaled * normal, -1, keepdims=True))
    return (grad_values, grad_gain)


def attention_scores(queries, keys, allowed):
    raw_scores = jnp.einsum("sihe,sjhe->shij", queries, keys, preferred_element_type=jnp.float32)
    return jnp.where(allowed, raw_scores * HS ** (-0.5), NEGATIVE)


def body(
    rows,
    lengths,
    freq_class,
    freq_table,
    gain_attn,
    gain_mlp,
    w_qkv,
    w_out,
    w_gate_up,
    w_down,
    cotangent,
):
    local_rows = rows.shape[0]
    mp_index = lax.axis_index("mp")
    series_count = lengths.shape[0]
    group_rows = series_count * SEQ
    heads_width = w_out.shape[0]
    head_count = heads_width // HS
    valid_mask, cosines, sines = series_tables(lengths)
    allowed = allowed_pairs(valid_mask)
    flat_valid = valid_mask.reshape(group_rows).astype(jnp.float32)
    mine_valid = lax.dynamic_slice_in_dim(flat_valid, mp_index * local_rows, local_rows)[:, None]
    classes = jnp.repeat(freq_class, SEQ)
    onehot = (classes[:, None] == jnp.arange(NFREQ, dtype=jnp.int32)[None, :]).astype(jnp.float32)
    start_rows = rows + jnp.dot(onehot, freq_table, precision=HIGHEST)
    normed_mine, inverse_attn = norm_forward(start_rows, gain_attn)
    normed = lax.all_gather(normed_mine, "mp", axis=0, tiled=True)
    qkv_low = w_qkv.astype(jnp.bfloat16)
    projected = jnp.einsum("td,cdf->ctf", normed, qkv_low, preferred_element_type=jnp.float32)
    projected = projected.reshape(3, series_count, SEQ, head_count, HS)
    queries = rotate(projected[0], cosines, sines).astype(jnp.bfloat16)
    keys = rotate(projected[1], cosines, sines).astype(jnp.bfloat16)
    values = projected[2].astype(jnp.bfloat16)
    scores = attention_scores(queries, keys, allowed)
    row_max = jnp.max(scores, -1, keepdims=True)
    exponent = jnp.exp(scores - row_max)
    row_total = jnp.sum(exponent, -1, keepdims=True)
    log_total = row_max + jnp.log(row_total)
    attention = (exponent / row_total).astype(jnp.bfloat16)
    mixed = jnp.einsum("shij,sjhe->sihe", attention, values, preferred_element_type=jnp.float32)
    mixed = mixed.reshape(group_rows, heads_width).astype(jnp.bfloat16)
    out_low = w_out.astype(jnp.bfloat16)
    attn_part = jnp.dot(mixed, out_low, preferred_element_type=jnp.float32)
    after_attn = start_rows + lax.psum_scatter(
        attn_part.astype(jnp.bfloat16), "mp", scatter_dimension=0, tiled=True
    ).astype(jnp.float32)
    normed_mlp_mine, inverse_mlp = norm_forward(after_attn, gain_mlp)
    normed_mlp = lax.all_gather(normed_mlp_mine, "mp", axis=0, tiled=True)
    gate_up_low = w_gate_up.astype(jnp.bfloat16)
    gate_up = jnp.einsum("td,cdf->ctf", normed_mlp, gate_up_low, preferred_element_type=jnp.float32)
    gate_pre = gate_up[0]
    up_pre = gate_up[1]
    sigmoid_gate = jax.nn.sigmoid(gate_pre)
    activated = gate_pre * sigmoid_gate
    hidden = (activated * up_pre).astype(jnp.bfloat16)
    down_low = w_down.astype(jnp.bfloat16)
    mlp_part = jnp.dot(hidden, down_low, preferred_element_type=jnp.float32)
    output = after_attn + lax.psum_scatter(
        mlp_part.astype(jnp.bfloat16), "mp", scatter_dimension=0, tiled=True
    ).astype(jnp.float32)
    grad_output = cotangent * mine_valid
    grad_down_in = lax.all_gather(grad_output.astype(jnp.bfloat16), "mp", axis=0, tiled=True)
    grad_down = jnp.einsum("tf,td->fd", hidden, grad_down_in, preferred_element_type=jnp.float32)
    grad_hidden = jnp.einsum(
        "td,fd->tf", grad_down_in, down_low, preferred_element_type=jnp.float32
    )
    grad_gate = grad_hidden * up_pre * (sigmoid_gate * (1.0 + gate_pre * (1.0 - sigmoid_gate)))
    grad_up = grad_hidden * activated
    grad_pre = jnp.stack([grad_gate, grad_up]).astype(jnp.bfloat16)
    grad_gate_up = jnp.einsum(
        "td,ctf->cdf", normed_mlp, grad_pre, preferred_element_type=jnp.float32
    )
    mlp_back_part = jnp.einsum(
        "ctf,cdf->td", grad_pre, gate_up_low, preferred_element_type=jnp.float32
    )
    grad_normed_mlp = lax.psum_scatter(
        mlp_back_part.astype(jnp.bfloat16), "mp", scatter_dimension=0, tiled=True
    ).astype(jnp.float32)
    grad_rows_mlp, grad_gain_mlp = norm_backward(after_attn, inverse_mlp, gain_mlp, grad_normed_mlp)
    grad_after = grad_output + grad_rows_mlp
    grad_attn_in = lax.all_gather(grad_after.astype(jnp.bfloat16), "mp", axis=0, tiled=True)
    grad_out = jnp.einsum("tf,td->fd", mixed, grad_attn_in, preferred_element_type=jnp.float32)
    grad_mixed = jnp.einsum("td,fd->tf", grad_attn_in, out_low, preferred_element_type=jnp.float32)
    grad_mixed = grad_mixed.astype(jnp.bfloat16).reshape(series_count, SEQ, head_count, HS)
    attention_again = jnp.exp(attention_scores(queries, keys, allowed) - log_total)
    grad_attention = jnp.einsum(
        "sihe,sjhe->shij", grad_mixed, values, preferred_element_type=jnp.float32
    )
    grad_values = jnp.einsum(
        "shij,sihe->sjhe",
        attention_again.astype(jnp.bfloat16),
        grad_mixed,
        preferred_element_type=jnp.float32,
    )
    row_dot = jnp.sum(attention_again * grad_attention, -1, keepdims=True)
    grad_scores = (attention_again * (grad_attention - row_dot)).astype(jnp.bfloat16)
    grad_queries = jnp.einsum(
        "shij,sjhe->sihe", grad_scores, keys, preferred_element_type=jnp.float32
    ) * HS ** (-0.5)
    grad_keys = jnp.einsum(
        "shij,sihe->sjhe", grad_scores, queries, preferred_element_type=jnp.float32
    ) * HS ** (-0.5)
    grad_projected = jnp.stack(
        [rotate(grad_queries, cosines, -sines), rotate(grad_keys, cosines, -sines), grad_values]
    )
    grad_projected = grad_projected.reshape(3, group_rows, heads_width).astype(jnp.bfloat16)
    grad_qkv = jnp.einsum("td,ctf->cdf", normed, grad_projected, preferred_element_type=jnp.float32)
    attn_back_part = jnp.einsum(
        "ctf,cdf->td", grad_projected, qkv_low, preferred_element_type=jnp.float32
    )
    grad_normed = lax.psum_scatter(
        attn_back_part.astype(jnp.bfloat16), "mp", scatter_dimension=0, tiled=True
    ).astype(jnp.float32)
    grad_rows_attn, grad_gain_attn = norm_backward(start_rows, inverse_attn, gain_attn, grad_normed)
    grad_rows = grad_after + grad_rows_attn
    grad_table = jnp.dot(onehot.T, grad_rows, precision=HIGHEST)
    grad_gain_attn, grad_gain_mlp, grad_table, token_total = lax.psum(
        (grad_gain_attn, grad_gain_mlp, grad_table, jnp.sum(mine_valid)), ("dp", "mp")
    )
    grad_qkv, grad_out, grad_gate_up, grad_down = (
        lax.psum(grad_qkv.astype(jnp.bfloat16), "dp").astype(jnp.float32),
        lax.psum(grad_out.astype(jnp.bfloat16), "dp").astype(jnp.float32),
        lax.psum(grad_gate_up.astype(jnp.bfloat16), "dp").astype(jnp.float32),
        lax.psum(grad_down.astype(jnp.bfloat16), "dp").astype(jnp.float32),
    )
    root_scale = lax.rsqrt(token_total)
    return (
        output,
        grad_rows,
        grad_qkv * root_scale,
        grad_out * root_scale,
        grad_gate_up * root_scale,
        grad_down * root_scale,
        grad_gain_attn * root_scale,
        grad_gain_mlp * root_scale,
        grad_table * root_scale,
    )


def solution(mesh):
    return jax.shard_map(
        body,
        mesh=mesh,
        in_specs=(
            P(("dp", "mp"), None),
            P("dp"),
            P(("dp", "mp")),
            P(),
            P(),
            P(),
            P(None, None, "mp"),
            P("mp", None),
            P(None, None, "mp"),
            P("mp", None),
            P(("dp", "mp"), None),
        ),
        out_specs=(
            P(("dp", "mp"), None),
            P(("dp", "mp"), None),
            P(None, None, "mp"),
            P("mp", None),
            P(None, None, "mp"),
            P("mp", None),
            P(),
            P(),
            P(),
        ),
        check_vma=False,
    )
```

profile of v0, /device:TPU:0, one launch (start us, length us, event | category | flops | bytes accessed | tf_op | source)
XLA Modules:
  0.0 1067.2 jit_solution(17084121526547978977)
XLA Ops:
  8.1 3.2 multiply_reduce_fusion.2
  13.6 5.8 fusion.48
  19.4 36.9 %all-gather.5.cloned.1.call-done = bf16[2048,1280]{1,0:T(8,128)(2,1)} async-done(((bf16[512,1280]{1,0:T(8,128)(2,1)}), bf16[2048,1280]{1,0:T(8,128)(2,1)}) %all-gather.5.cloned.1.call-update) | async-done | bytes 5242896 | tf_op jit(solution)/shard_map/all_gather | solution.py:85
  56.3 8.7 fusion.10
  69.2 4.9 reshape.176
  74.1 4.7 copy.39
  78.8 5.3 reshape.177
  84.1 5.5 fusion.62
  89.6 4.9 copy.73
  94.5 4.9 copy.72
  99.3 5.3 reshape.178
  104.7 5.5 fusion.63
  110.1 4.9 copy.75
  115.0 4.9 copy.74
  119.9 7.9 subtract_convert_fusion.3
  135.5 3.3 copy.41
  138.7 4.3 convert_element_type.131
  143.1 7.1 convolution_convert_fusion.2
  150.3 51.5 %reduce-scatter.5.cloned.1.call-done = bf16[512,1280]{1,0:T(8,128)(2,1)} async-done(((bf16[2048,1280]{1,0:T(8,128)(2,1)}), bf16[512,1280]{1,0:T(8,128)(2,1)}) %reduce-scatter.5.cloned.1.call-update) | async-done | bytes 1310736 | tf_op jit(solution)/shard_map/reduce_scatter | solution.py:102
  208.6 38.5 %all-gather.7.cloned.1.call-done = bf16[2048,1280]{1,0:T(8,128)(2,1)} async-done(((bf16[512,1280]{1,0:T(8,128)(2,1)}), bf16[2048,1280]{1,0:T(8,128)(2,1)}) %all-gather.7.cloned.1.call-update) | async-done | bytes 5242896 | tf_op jit(solution)/shard_map/all_gather | solution.py:106
  247.0 22.6 %convolution_bitcast_fusion = f32[2,2048,1280]{2,1,0:T(8,128)} fusion(bf16[2048,1280]{1,0:T(8,128)(2,1)} %all-gather.7.cloned.1.call-done, f32[2,1280,1280]{2,1,0:T(8,128)} %param.19), kind=kOutput, calls=%fused_computation.1 | convolution fusion | flops 13425049600 | bytes 39321600 | tf_op jit(solution)/shard_map/td,cdf->ctf/dot_general | solution.py:108
  269.6 20.0 %all-gather.9.cloned.1.call-done = bf16[2048,1280]{1,0:T(8,128)(2,1)} async-done(((bf16[512,1280]{1,0:T(8,128)(2,1)}), bf16[2048,1280]{1,0:T(8,128)(2,1)}) %all-gather.9.cloned.1.call-update) | async-done | bytes 5242896 | tf_op jit(solution)/shard_map/all_gather | solution.py:120
  289.6 21.7 %fusion.9 = (bf16[1,2048,1280]{2,1,0:T(8,128)(2,1)}, bf16[1,2048,1280]{2,1,0:T(8,128)(2,1)}, bf16[2048,1280]{1,0:T(8,128)(2,1)}) fusion(f32[2,2048,1280]{2,1,0:T(8,128)} %convolution_bitcast_fusion, bf16[2048,1280]{1,0:T(8,128)(2,1)} %all-gather.9.cloned.1.call-done, f32[1280,1280]{1,0:T(8,128)} %param.20), kind=kOutput, calls=%fused_computation.25 | convolution fusion | flops 6751846400 | bytes 48496640 | tf_op jit(solution)/shard_map/td,fd->tf/dot_general | solution.py:122
  311.2 21.7 %bitcast_convert_fusion.1 = bf16[2048,1280]{1,0:T(8,128)(2,1)} fusion(bf16[1,2048,1280]{2,1,0:T(8,128)(2,1)} %get-tuple-element.46, bf16[1,2048,1280]{2,1,0:T(8,128)(2,1)} %get-tuple-element.45, f32[2,1280,1280]{2,1,0:T(8,128)} %param.19), kind=kOutput, calls=%fused_computation.7 | convolution fusion | flops 13432913920 | bytes 28835840 | tf_op jit(solution)/shard_map/ctf,cdf->td/dot_general | solution.py:131
  333.0 12.4 %convolution_convert_fusion.1 = bf16[2048,1280]{1,0:T(8,128)(2,1)} fusion(bf16[2048,1280]{1,0:T(8,128)(2,1)} %get-tuple-element.47, f32[1280,1280]{1,0:T(8,128)} %param.20), kind=kOutput, calls=%fused_computation.14 | convolution fusion | flops 6715146240 | bytes 17039360 | tf_op jit(solution)/shard_map/dot_general | solution.py:115
  345.4 39.1 %reduce-scatter.9.cloned.1.call-done = bf16[512,1280]{1,0:T(8,128)(2,1)} async-done(((bf16[2048,1280]{1,0:T(8,128)(2,1)}), bf16[512,1280]{1,0:T(8,128)(2,1)}) %reduce-scatter.9.cloned.1.call-update) | async-done | bytes 1310736 | tf_op jit(solution)/shard_map/reduce_scatter | solution.py:134
  386.7 51.7 %reduce-scatter.7.cloned.1.call-done = bf16[512,1280]{1,0:T(8,128)(2,1)} async-done(((bf16[2048,1280]{1,0:T(8,128)(2,1)}), bf16[512,1280]{1,0:T(8,128)(2,1)}) %reduce-scatter.7.cloned.1.call-update) | async-done | bytes 1310736 | tf_op jit(solution)/shard_map/reduce_scatter | solution.py:116
  438.4 6.3 fusion.59
  444.8 40.5 %all-gather.11.cloned.1.call-done = bf16[2048,1280]{1,0:T(8,128)(2,1)} async-done(((bf16[512,1280]{1,0:T(8,128)(2,1)}), bf16[2048,1280]{1,0:T(8,128)(2,1)}) %all-gather.11.cloned.1.call-update) | async-done | bytes 5242896 | tf_op jit(solution)/shard_map/all_gather | solution.py:139
  485.3 4.9 convolution_convert_fusion.5
  490.2 4.0 reshape.179
  494.2 3.6 copy.43
  497.8 4.5 convert_bitcast_fusion
  509.9 4.7 subtract_convert_fusion
  517.1 5.0 copy.59
  525.2 5.0 copy.60
  533.0 4.7 pad_maximum_fusion.5
  537.7 5.0 copy.58
  550.5 9.9 bitcast_convert_fusion
  560.5 12.3 %convolution_convert_fusion.3 = bf16[1280,1280]{1,0:T(8,128)(2,1)} fusion(bf16[2048,1280]{1,0:T(8,128)(2,1)} %get-tuple-element.47, bf16[2048,1280]{1,0:T(8,128)(2,1)} %all-gather.9.cloned.1.call-done), kind=kOutput, calls=%fused_computation.16 | convolution fusion | flops 6712524800 | bytes 13762560 | tf_op jit(solution)/shard_map/tf,td->fd/dot_general | solution.py:121
  572.8 20.2 %fusion.1 = bf16[2,1280,1280]{1,2,0:T(8,128)(2,1)} fusion(bf16[1,2048,1280]{2,1,0:T(8,128)(2,1)} %get-tuple-element.46, bf16[1,2048,1280]{2,1,0:T(8,128)(2,1)} %get-tuple-element.45, bf16[2048,1280]{1,0:T(8,128)(2,1)} %all-gather.7.cloned.1.call-done), kind=kOutput, calls=%fused_computation.13 | convolution fusion | flops 13430292480 | bytes 22282240 | tf_op jit(solution)/shard_map/td,ctf->cdf/dot_general | solution.py:128
  595.9 6.5 fusion.20
  602.5 9.5 reduce-scatter.11.cloned.1.call-done
  617.7 44.2 %all-reduce = (f32[]{:T(128)}, f32[1280]{0:T(1024)S(1)}, f32[1280]{0:T(1024)S(1)}, f32[3,1280]{1,0:T(4,128)S(1)}) all-reduce(f32[]{:T(128)} %get-tuple-element.39, f32[1280]{0:T(1024)S(1)} %get-tuple-element.29, f32[1280]{0:T(1024)S(1)} %get-tuple-element.27, f32[3,1280]{1,0:T(4,128)S(1)} %fusion.49), channel_id=1, replica_groups=mesh['dp'=8,'mp'=4] {'dp','mp'}, use_global_device_ids=true, to_apply=%region_13.14 | all-reduce | flops 6401 | bytes 51208 | tf_op jit(solution)/shard_map/psum | solution.py:175
  664.4 365.7 %all-reduce.4.cloned.1.call-done = (bf16[3,1280,320]{1,2,0:T(8,128)(2,1)}, bf16[320,1280]{1,0:T(8,128)(2,1)}, bf16[2,1280,1280]{1,2,0:T(8,128)(2,1)}, bf16[1280,1280]{1,0:T(8,128)(2,1)}) async-done(((bf16[3,1280,320]{1,2,0:T(8,128)(2,1)}, bf16[320,1280]{1,0:T(8,128)(2,1)}, bf16[2,1280,1280]{1,2,0:T(8,128)(2,1)}, bf16[1280,1280]{1,0:T(8,128)(2,1)}), (bf16[3,1280,320]{1,2,0:T(8,128)(2,1)}, ...) | async-done | bytes 13107216 | tf_op jit(solution)/shard_map/psum | solution.py:179
  1036.0 3.7 convert_multiply_fusion.1
  1040.7 5.8 convert_multiply_fusion
  1046.5 13.9 %copy.54 = f32[2,1280,1280]{2,1,0:T(8,128)} copy(f32[2,1280,1280]{1,2,0:T(8,128)} %convert_multiply_fusion) | data formatting | bytes 26214400
  (154 shorter events, 65.1 us)
Async XLA Ops:
  7.2 4.1 copy-start.31
  7.2 49.1 %all-gather.5.cloned.1.call-start = ((), (), s32[]{:S(2)}) async-start(), calls=%async_computation.4 | async-start | bytes 6553600 | tf_op jit(solution)/shard_map/all_gather | solution.py:85
  8.1 4.9 copy-start.35
  11.3 190.5 %copy-start.4 = (f32[512,1280]{1,0:T(8,128)}, f32[512,1280]{1,0:T(8,128)S(1)}, u32[]{:S(2)}) copy-start(f32[512,1280]{1,0:T(8,128)S(1)} %get-tuple-element.73) | copy-start | bytes 7864324
  11.3 1.8 copy-start.37
  11.3 1.8 copy-start.33
  13.0 188.8 %reduce-scatter.5.cloned.1.call-start = ((), (), s32[]{:S(2)}) async-start(), calls=%async_computation.5 | async-start | bytes 6553600 | tf_op jit(solution)/shard_map/reduce_scatter | solution.py:102
  127.9 3.3 copy-start.8
  127.9 3.3 copy-start.10
  127.9 3.3 copy-start.12
  127.9 3.3 copy-start.14
  131.2 4.3 copy-start.2
  131.2 3.1 copy-start.20
  150.2 54.8 %copy-start.30 = (f32[1280]{0:T(1024)S(1)}, f32[1280]{0:T(1024)}, u32[]{:S(2)}) copy-start(f32[1280]{0:T(1024)} %param.16) | copy-start | bytes 15364
  150.2 96.8 %all-gather.7.cloned.1.call-start = ((), (), s32[]{:S(2)}) async-start(), calls=%async_computation.6 | async-start | bytes 6553600 | tf_op jit(solution)/shard_map/all_gather | solution.py:106
  203.6 3.7 copy-start.18
  206.4 83.1 %all-gather.9.cloned.1.call-start = ((), (), s32[]{:S(2)}) async-start(), calls=%async_computation.8 | async-start | bytes 6553600 | tf_op jit(solution)/shard_map/all_gather | solution.py:120
  208.5 176.0 %reduce-scatter.9.cloned.1.call-start = ((), (), s32[]{:S(2)}) async-start(), calls=%async_computation.9 | async-start | bytes 6553600 | tf_op jit(solution)/shard_map/reduce_scatter | solution.py:134
  333.0 105.4 %reduce-scatter.7.cloned.1.call-start = ((), (), s32[]{:S(2)}) async-start(), calls=%async_computation.7 | async-start | bytes 6553600 | tf_op jit(solution)/shard_map/reduce_scatter | solution.py:116
  345.4 39.1 %copy-start.7 = (f32[512,1280]{1,0:T(8,128)S(1)}, f32[512,1280]{1,0:T(8,128)}, u32[]{:S(2)}) copy-start(f32[512,1280]{1,0:T(8,128)} %copy-done.6) | copy-start | bytes 7864324
  345.4 139.9 %all-gather.11.cloned.1.call-start = ((), (), s32[]{:S(2)}) async-start(), calls=%async_computation.10 | async-start | bytes 6553600 | tf_op jit(solution)/shard_map/all_gather | solution.py:139
  444.7 167.3 %reduce-scatter.11.cloned.1.call-start = ((), (), s32[]{:S(2)}) async-start(), calls=%async_computation.11 | async-start | bytes 6553600 | tf_op jit(solution)/shard_map/reduce_scatter | solution.py:169
  497.8 4.5 copy-start.3
  497.8 4.5 copy-start.21
  503.7 2.2 copy-start.15
  505.9 2.2 copy-start.11
  508.1 1.8 copy-start.19
  508.1 1.8 copy-start.24
  545.5 2.9 copy-start.23
  548.5 1.9 copy-start.28
  560.4 469.8 %all-reduce.4.cloned.1.call-start = ((), (), s32[]{:S(2)}) async-start(), calls=%async_computation.12 | async-start | bytes 26214400 | tf_op jit(solution)/shard_map/psum | solution.py:179
  560.4 32.6 %slice-start.4 = ((s8[5242880]{0:T(1024)(128)(4,1)}), s8[4194304]{0:T(1024)(128)(4,1)S(1)}, s32[]{:S(2)}) async-start(s8[5242880]{0:T(1024)(128)(4,1)} %bitcast.110), calls=%async_computation.17 | async-start | bytes 8388608
  560.5 35.5 %slice-start.2 = ((s8[5242880]{0:T(1024)(128)(4,1)}), s8[4194304]{0:T(1024)(128)(4,1)S(1)}, s32[]{:S(2)}) async-start(s8[5242880]{0:T(1024)(128)(4,1)} %bitcast.108), calls=%async_computation.15 | async-start | bytes 8388608
  572.8 20.3 %copy-start.27 = (bf16[2048,320]{1,0:T(8,128)(2,1)S(1)}, bf16[2048,320]{1,0:T(8,128)(2,1)}, u32[]{:S(2)}) copy-start(bf16[2048,320]{1,0:T(8,128)(2,1)} %convert_element_type.131) | copy-start | bytes 3932164
  572.8 20.3 %slice-start.5 = ((s8[5242880]{0:T(1024)(128)(4,1)}), s8[1048576]{0:T(1024)(128)(4,1)S(1)}, s32[]{:S(2)}) async-start(s8[5242880]{0:T(1024)(128)(4,1)} %bitcast.110), calls=%async_computation.18 | async-start | bytes 2097152
  572.8 23.1 %slice-start.3 = ((s8[5242880]{0:T(1024)(128)(4,1)}), s8[1048576]{0:T(1024)(128)(4,1)S(1)}, s32[]{:S(2)}) async-start(s8[5242880]{0:T(1024)(128)(4,1)} %bitcast.108), calls=%async_computation.16 | async-start | bytes 2097152
  593.1 2.8 copy-start.29
  602.5 9.5 copy-start.5
  602.5 9.5 copy-start.32
  602.5 9.5 copy-start.34
  612.0 2.3 copy-start.17
  612.0 2.5 copy-start.22
  614.5 2.2 copy-start.36
  1030.2 2.6 copy-start.26
  1032.7 3.3 copy-start.25
  1032.7 7.0 slice-start
  1036.0 4.7 slice-start.1
  1046.5 13.9 %copy-start.1 = (f32[3,1280]{1,0:T(4,128)S(1)}, f32[3,1280]{1,0:T(4,128)}, u32[]{:S(2)}) copy-start(f32[3,1280]{1,0:T(4,128)} %param.14) | copy-start | bytes 46084
  (5 other events, 7.1 us)
Sparse Core Ops, SparseCore 0:
  13.1 43.1 all-gather.4
  150.3 51.3 reduce-scatter.4
  206.5 40.4 all-gather.6
  249.1 40.4 all-gather.8
  333.1 51.3 reduce-scatter.8
  386.9 51.3 reduce-scatter.6
  444.8 40.4 all-gather.10
  560.5 51.3 reduce-scatter.10
  617.3 412.7 all-reduce.3
where the time goes:
time: 1080 us; the launch traced here: 1070 us
  waiting for transfers between devices  653 us (60%)
  matrix products  168 us (16%)
  local copies, waits for them, and re-layouts  122 us (11%)
  other arithmetic  63.7 us (6%)
  blocking collectives  44.2 us (4%)
  between operations  15.3 us (1%)
    psum x1, waiting for transfers between devices, body(): lax.psum(grad_qkv.astype(jnp.bfloat16), 'dp').astype(jnp.float32)  366 us
    reduce_scatter x1, waiting for transfers between devices, body(): lax.psum_scatter(mlp_part.astype(jnp.bfloat16), 'mp', scatter_dimension=0...  51.7 us
    reduce_scatter x1, waiting for transfers between devices, body(): lax.psum_scatter(attn_part.astype(jnp.bfloat16), 'mp', scatter_dimension=...  51.5 us
    unnamed x95, local copies, waits for them, and re-layouts  46.5 us
    psum x1, blocking collectives, body(): lax.psum((grad_gain_attn, grad_gain_mlp, grad_table, jnp.sum(mine_valid))...  44.2 us
    all_gather x1, waiting for transfers between devices, body(): lax.all_gather(grad_after.astype(jnp.bfloat16), 'mp', axis=0, tiled=True)  40.5 us
    reduce_scatter x1, waiting for transfers between devices, body(): lax.psum_scatter(mlp_back_part.astype(jnp.bfloat16), 'mp', scatter_dimens...  39.1 us
    all_gather x1, waiting for transfers between devices, body(): normed_mlp = lax.all_gather(normed_mlp_mine, 'mp', axis=0, tiled=True)  38.5 us
  transfers between devices with their start and end apart: 9, of which 9 were waited for; matrix products, arithmetic and copies ran while one was open for 9% of the time, Pallas kernels for 0%

commit v1 on v0

--- a/solution.py
+++ b/solution.py
@@ -176,7 +176,7 @@
         (grad_gain_attn, grad_gain_mlp, grad_table, jnp.sum(mine_valid)), ("dp", "mp")
     )
     grad_qkv, grad_out, grad_gate_up, grad_down = (
-        lax.psum(grad_qkv.astype(jnp.bfloat16), "dp").astype(jnp.float32),
+        jnp.sum(lax.all_gather(grad_qkv.astype(jnp.bfloat16), "dp"), axis=0).astype(jnp.float32),
         lax.psum(grad_out.astype(jnp.bfloat16), "dp").astype(jnp.float32),
         lax.psum(grad_gate_up.astype(jnp.bfloat16), "dp").astype(jnp.float32),
         lax.psum(grad_down.astype(jnp.bfloat16), "dp").astype(jnp.float32),

time: 1080 us -> 1360 us (1.26)
  waiting for transfers between devices: 653 us -> 920 us
    all_gather x0 -> x1, waiting for transfers between devices: none -> 349 us  [body(): lax.all_gather(grad_qkv.astype(jnp.bfloat16), 'dp')]
    psum x1, waiting for transfers between devices: 366 us -> 287 us  [body(): lax.psum(grad_out.astype(jnp.bfloat16), 'dp').astype(jnp.float32)]
    unnamed x95 -> x83, local copies, waits for them, and re-layouts: 46.5 us -> 45.3 us
  transfers between devices with their start and end apart: 9 -> 10, of which waited for: 9 -> 10; matrix products, arithmetic and copies ran while one was open for 9% -> 9% of each run, Pallas kernels for 0% -> 0%
where the time goes in v1:
time: 1360 us; the launch traced here: 1350 us
  waiting for transfers between devices  920 us (68%)
  matrix products  172 us (13%)
  local copies, waits for them, and re-layouts  120 us (9%)
  other arithmetic  77.1 us (6%)
  blocking collectives  44.6 us (3%)
  between operations  15.6 us (1%)
    all_gather x1, waiting for transfers between devices, body(): lax.all_gather(grad_qkv.astype(jnp.bfloat16), 'dp')  349 us
    psum x1, waiting for transfers between devices, body(): lax.psum(grad_out.astype(jnp.bfloat16), 'dp').astype(jnp.float32)  287 us
    reduce_scatter x1, waiting for transfers between devices, body(): lax.psum_scatter(mlp_part.astype(jnp.bfloat16), 'mp', scatter_dimension=0...  51.7 us
    reduce_scatter x1, waiting for transfers between devices, body(): lax.psum_scatter(attn_part.astype(jnp.bfloat16), 'mp', scatter_dimension=...  51.5 us
    unnamed x83, local copies, waits for them, and re-layouts  45.3 us
    psum x1, blocking collectives, body(): lax.psum((grad_gain_attn, grad_gain_mlp, grad_table, jnp.sum(mine_valid))...  44.6 us
    all_gather x1, waiting for transfers between devices, body(): lax.all_gather(grad_after.astype(jnp.bfloat16), 'mp', axis=0, tiled=True)  40.5 us
    reduce_scatter x1, waiting for transfers between devices, body(): lax.psum_scatter(mlp_back_part.astype(jnp.bfloat16), 'mp', scatter_dimens...  39.1 us
  transfers between devices with their start and end apart: 10, of which 10 were waited for; matrix products, arithmetic and copies ran while one was open for 9% of the time, Pallas kernels for 0%

profile of v1, /device:TPU:0, one launch (start us, length us, event | category | flops | bytes accessed | tf_op | source)
XLA Modules:
  0.0 1350.0 jit_solution(5364075509722360053)
XLA Ops:
  13.6 5.8 fusion.48
  19.4 36.9 %all-gather.7.cloned.1.call-done = bf16[2048,1280]{1,0:T(8,128)(2,1)} async-done(((bf16[512,1280]{1,0:T(8,128)(2,1)}), bf16[2048,1280]{1,0:T(8,128)(2,1)}) %all-gather.7.cloned.1.call-update) | async-done | bytes 5242896 | tf_op jit(solution)/shard_map/all_gather | solution.py:85
  56.2 8.7 fusion.10
  69.2 4.9 reshape.177
  74.1 4.6 copy.62
  78.7 5.3 reshape.178
  84.0 5.5 fusion.62
  89.5 4.9 copy.96
  94.4 4.9 copy.95
  99.2 5.3 reshape.179
  104.6 5.5 fusion.63
  110.0 4.9 copy.98
  115.0 4.9 copy.97
  119.8 8.0 subtract_convert_fusion.3
  135.4 3.3 copy.64
  138.7 4.3 convert_element_type.133
  143.0 7.1 convolution_convert_fusion.2
  150.2 51.5 %reduce-scatter.5.cloned.1.call-done = bf16[512,1280]{1,0:T(8,128)(2,1)} async-done(((bf16[2048,1280]{1,0:T(8,128)(2,1)}), bf16[512,1280]{1,0:T(8,128)(2,1)}) %reduce-scatter.5.cloned.1.call-update) | async-done | bytes 1310736 | tf_op jit(solution)/shard_map/reduce_scatter | solution.py:102
  208.5 38.5 %all-gather.9.cloned.1.call-done = bf16[2048,1280]{1,0:T(8,128)(2,1)} async-done(((bf16[512,1280]{1,0:T(8,128)(2,1)}), bf16[2048,1280]{1,0:T(8,128)(2,1)}) %all-gather.9.cloned.1.call-update) | async-done | bytes 5242896 | tf_op jit(solution)/shard_map/all_gather | solution.py:106
  246.9 22.6 %convolution_bitcast_fusion = f32[2,2048,1280]{2,1,0:T(8,128)} fusion(bf16[2048,1280]{1,0:T(8,128)(2,1)} %all-gather.9.cloned.1.call-done, f32[2,1280,1280]{2,1,0:T(8,128)} %param.19), kind=kOutput, calls=%fused_computation.1 | convolution fusion | flops 13425049600 | bytes 39321600 | tf_op jit(solution)/shard_map/td,cdf->ctf/dot_general | solution.py:108
  269.5 19.9 %all-gather.11.cloned.1.call-done = bf16[2048,1280]{1,0:T(8,128)(2,1)} async-done(((bf16[512,1280]{1,0:T(8,128)(2,1)}), bf16[2048,1280]{1,0:T(8,128)(2,1)}) %all-gather.11.cloned.1.call-update) | async-done | bytes 5242896 | tf_op jit(solution)/shard_map/all_gather | solution.py:120
  289.5 21.7 %fusion.9 = (bf16[1,2048,1280]{2,1,0:T(8,128)(2,1)}, bf16[1,2048,1280]{2,1,0:T(8,128)(2,1)}, bf16[2048,1280]{1,0:T(8,128)(2,1)}) fusion(f32[2,2048,1280]{2,1,0:T(8,128)} %convolution_bitcast_fusion, bf16[2048,1280]{1,0:T(8,128)(2,1)} %all-gather.11.cloned.1.call-done, f32[1280,1280]{1,0:T(8,128)} %param.20), kind=kOutput, calls=%fused_computation.25 | convolution fusion | flops 6751846400 | bytes 48496640 | tf_op jit(solution)/shard_map/td,fd->tf/dot_general | solution.py:122
  311.1 21.7 %bitcast_convert_fusion.1 = bf16[2048,1280]{1,0:T(8,128)(2,1)} fusion(bf16[1,2048,1280]{2,1,0:T(8,128)(2,1)} %get-tuple-element.54, bf16[1,2048,1280]{2,1,0:T(8,128)(2,1)} %get-tuple-element.53, f32[2,1280,1280]{2,1,0:T(8,128)} %param.19), kind=kOutput, calls=%fused_computation.7 | convolution fusion | flops 13432913920 | bytes 28835840 | tf_op jit(solution)/shard_map/ctf,cdf->td/dot_general | solution.py:131
  332.9 12.4 convolution_convert_fusion.1
  345.4 39.1 %reduce-scatter.9.cloned.1.call-done = bf16[512,1280]{1,0:T(8,128)(2,1)} async-done(((bf16[2048,1280]{1,0:T(8,128)(2,1)}), bf16[512,1280]{1,0:T(8,128)(2,1)}) %reduce-scatter.9.cloned.1.call-update) | async-done | bytes 1310736 | tf_op jit(solution)/shard_map/reduce_scatter | solution.py:134
  386.6 51.7 %reduce-scatter.7.cloned.1.call-done = bf16[512,1280]{1,0:T(8,128)(2,1)} async-done(((bf16[2048,1280]{1,0:T(8,128)(2,1)}), bf16[512,1280]{1,0:T(8,128)(2,1)}) %reduce-scatter.7.cloned.1.call-update) | async-done | bytes 1310736 | tf_op jit(solution)/shard_map/reduce_scatter | solution.py:116
  438.2 6.3 fusion.59
  444.6 40.5 %all-gather.13.cloned.1.call-done = bf16[2048,1280]{1,0:T(8,128)(2,1)} async-done(((bf16[512,1280]{1,0:T(8,128)(2,1)}), bf16[2048,1280]{1,0:T(8,128)(2,1)}) %all-gather.13.cloned.1.call-update) | async-done | bytes 5242896 | tf_op jit(solution)/shard_map/all_gather | solution.py:139
  485.1 4.9 convolution_convert_fusion.5
  490.0 3.9 reshape.180
  494.0 3.6 copy.66
  497.6 4.5 convert_bitcast_fusion
  509.8 4.7 subtract_convert_fusion
  517.0 5.0 copy.82
  525.1 5.0 copy.83
  533.0 4.8 pad_maximum_fusion.5
  537.7 5.0 copy.81
  550.5 10.0 bitcast_convert_fusion
  560.6 12.4 convolution_convert_fusion.3
  573.0 20.2 %fusion.1 = bf16[2,1280,1280]{1,2,0:T(8,128)(2,1)} fusion(bf16[1,2048,1280]{2,1,0:T(8,128)(2,1)} %get-tuple-element.54, bf16[1,2048,1280]{2,1,0:T(8,128)(2,1)} %get-tuple-element.53, bf16[2048,1280]{1,0:T(8,128)(2,1)} %all-gather.9.cloned.1.call-done), kind=kOutput, calls=%fused_computation.13 | convolution fusion | flops 13430292480 | bytes 22282240 | tf_op jit(solution)/shard_map/td,ctf->cdf/dot_general | solution.py:128
  596.2 9.9 fusion.20
  606.0 6.0 reduce-scatter.11.cloned.1.call-done
  617.8 44.6 %all-reduce = (f32[]{:T(128)}, f32[1280]{0:T(1024)S(1)}, f32[1280]{0:T(1024)S(1)}, f32[3,1280]{1,0:T(4,128)S(1)}) all-reduce(f32[]{:T(128)} %get-tuple-element.47, f32[1280]{0:T(1024)S(1)} %get-tuple-element.38, f32[1280]{0:T(1024)S(1)} %get-tuple-element.36, f32[3,1280]{1,0:T(4,128)S(1)} %fusion.49), channel_id=1, replica_groups=mesh['dp'=8,'mp'=4] {'dp','mp'}, use_global_device_ids=true, to_apply=%region_13.14 | all-reduce | flops 6401 | bytes 51208 | tf_op jit(solution)/shard_map/psum | solution.py:175
  664.9 286.8 %all-reduce.4.cloned.1.call-done = (bf16[320,1280]{1,0:T(8,128)(2,1)}, bf16[2,1280,1280]{1,2,0:T(8,128)(2,1)}, bf16[1280,1280]{1,0:T(8,128)(2,1)}) async-done(((bf16[320,1280]{1,0:T(8,128)(2,1)}, bf16[2,1280,1280]{1,2,0:T(8,128)(2,1)}, bf16[1280,1280]{1,0:T(8,128)(2,1)}), (bf16[320,1280]{1,0:T(8,128)(2,1)}, bf16[2,1280,1280]{1,2,0:T(8,128)(2,1)}, bf16[1280,1280]{1,0:T(8,128)(2,1)})) %all-reduce.4.cloned.1.call-update) | async-done | bytes 10649616 | tf_op jit(solution)/shard_map/psum | solution.py:180
  951.8 9.1 convert_multiply_fusion
  960.8 14.1 %copy.77 = f32[2,1280,1280]{2,1,0:T(8,128)} copy(f32[2,1280,1280]{1,2,0:T(8,128)} %convert_multiply_fusion) | data formatting | bytes 26214400
  980.5 348.8 %all-gather.15.cloned.1.call-done = bf16[24,1280,320]{1,2,0:T(8,128)(2,1)} async-done(((bf16[3,1280,320]{1,2,0:T(8,128)(2,1)}), bf16[24,1280,320]{1,2,0:T(8,128)(2,1)}) %all-gather.15.cloned.1.call-update) | async-done | bytes 19660816 | tf_op jit(solution)/shard_map/all_gather | solution.py:179
  1329.3 10.9 reduce_sum.99
  (144 shorter events, 69.8 us)
Async XLA Ops:
  7.2 0.9 copy-start
  7.2 4.1 copy-start.29
  7.2 49.0 %all-gather.7.cloned.1.call-start = ((), (), s32[]{:S(2)}) async-start(), calls=%async_computation.4 | async-start | bytes 6553600 | tf_op jit(solution)/shard_map/all_gather | solution.py:85
  8.1 4.9 copy-start.33
  11.3 190.4 %copy-start.4 = (f32[512,1280]{1,0:T(8,128)}, f32[512,1280]{1,0:T(8,128)S(1)}, u32[]{:S(2)}) copy-start(f32[512,1280]{1,0:T(8,128)S(1)} %get-tuple-element.81) | copy-start | bytes 7864324
  11.3 1.8 copy-start.35
  11.3 1.7 copy-start.31
  12.9 188.8 %reduce-scatter.5.cloned.1.call-start = ((), (), s32[]{:S(2)}) async-start(), calls=%async_computation.5 | async-start | bytes 6553600 | tf_op jit(solution)/shard_map/reduce_scatter | solution.py:102
  127.8 3.3 copy-start.8
  127.8 3.3 copy-start.10
  127.8 3.3 copy-start.12
  127.8 3.3 copy-start.14
  131.1 4.3 copy-start.2
  131.1 3.1 copy-start.20
  150.2 54.8 %copy-start.28 = (f32[1280]{0:T(1024)S(1)}, f32[1280]{0:T(1024)}, u32[]{:S(2)}) copy-start(f32[1280]{0:T(1024)} %param.16) | copy-start | bytes 15364
  150.2 96.8 %all-gather.9.cloned.1.call-start = ((), (), s32[]{:S(2)}) async-start(), calls=%async_computation.6 | async-start | bytes 6553600 | tf_op jit(solution)/shard_map/all_gather | solution.py:106
  203.5 1.5 copy-start.6
  203.5 3.7 copy-start.18
  206.3 83.1 %all-gather.11.cloned.1.call-start = ((), (), s32[]{:S(2)}) async-start(), calls=%async_computation.8 | async-start | bytes 6553600 | tf_op jit(solution)/shard_map/all_gather | solution.py:120
  208.4 176.0 %reduce-scatter.9.cloned.1.call-start = ((), (), s32[]{:S(2)}) async-start(), calls=%async_computation.9 | async-start | bytes 6553600 | tf_op jit(solution)/shard_map/reduce_scatter | solution.py:134
  332.9 105.4 %reduce-scatter.7.cloned.1.call-start = ((), (), s32[]{:S(2)}) async-start(), calls=%async_computation.7 | async-start | bytes 6553600 | tf_op jit(solution)/shard_map/reduce_scatter | solution.py:116
  345.3 39.1 %copy-start.7 = (f32[512,1280]{1,0:T(8,128)S(1)}, f32[512,1280]{1,0:T(8,128)}, u32[]{:S(2)}) copy-start(f32[512,1280]{1,0:T(8,128)} %copy-done.6) | copy-start | bytes 7864324
  345.3 139.8 %all-gather.13.cloned.1.call-start = ((), (), s32[]{:S(2)}) async-start(), calls=%async_computation.10 | async-start | bytes 6553600 | tf_op jit(solution)/shard_map/all_gather | solution.py:139
  444.5 167.5 %reduce-scatter.11.cloned.1.call-start = ((), (), s32[]{:S(2)}) async-start(), calls=%async_computation.11 | async-start | bytes 6553600 | tf_op jit(solution)/shard_map/reduce_scatter | solution.py:169
  497.6 4.6 copy-start.3
  497.6 4.5 copy-start.21
  503.5 1.6 copy-start.13
  503.6 2.2 copy-start.15
  505.8 1.6 copy-start.9
  505.8 2.2 copy-start.11
  508.0 1.8 copy-start.19
  508.0 1.8 copy-start.24
  545.6 2.9 copy-start.23
  548.6 1.9 copy-start.27
  560.5 391.2 %all-reduce.4.cloned.1.call-start = ((), (), s32[]{:S(2)}) async-start(), calls=%async_computation.13 | async-start | bytes 21299200 | tf_op jit(solution)/shard_map/psum | solution.py:180
  560.6 32.7 %slice-start = ((s8[5242880]{0:T(1024)(128)(4,1)}), s8[4194304]{0:T(1024)(128)(4,1)S(1)}, s32[]{:S(2)}) async-start(s8[5242880]{0:T(1024)(128)(4,1)} %bitcast.108), calls=%async_computation.14 | async-start | bytes 8388608
  573.0 20.3 %copy-start.26 = (bf16[2048,320]{1,0:T(8,128)(2,1)S(1)}, bf16[2048,320]{1,0:T(8,128)(2,1)}, u32[]{:S(2)}) copy-start(bf16[2048,320]{1,0:T(8,128)(2,1)} %convert_element_type.133) | copy-start | bytes 3932164
  573.0 20.3 %slice-start.1 = ((s8[5242880]{0:T(1024)(128)(4,1)}), s8[1048576]{0:T(1024)(128)(4,1)S(1)}, s32[]{:S(2)}) async-start(s8[5242880]{0:T(1024)(128)(4,1)} %bitcast.108), calls=%async_computation.15 | async-start | bytes 2097152
  596.1 16.0 %copy-start.30 = (f32[1280]{0:T(1024)S(1)}, f32[1280]{0:T(1024)}, u32[]{:S(2)}) copy-start(f32[1280]{0:T(1024)} %param.15) | copy-start | bytes 15364
  596.1 16.0 %copy-start.32 = (f32[512]{0:T(512)S(1)}, f32[512]{0:T(512)}, u32[]{:S(2)}) copy-start(f32[512]{0:T(512)} %copy-done.31) | copy-start | bytes 6148
  596.1 733.2 %all-gather.15.cloned.1.call-start = ((), (), s32[]{:S(2)}) async-start(), calls=%async_computation.12 | async-start | bytes 22118400 | tf_op jit(solution)/shard_map/all_gather | solution.py:179
  596.2 15.9 %copy-start.5 = (f32[512,1280]{1,0:T(8,128)S(1)}, f32[512,1280]{1,0:T(8,128)}, u32[]{:S(2)}) copy-start(f32[512,1280]{1,0:T(8,128)} %copy-done.4) | copy-start | bytes 7864324
  612.1 2.3 copy-start.17
  612.1 2.5 copy-start.22
  614.6 2.2 copy-start.34
  615.3 1.5 copy-start.16
  960.8 16.5 %copy-start.25 = (bf16[1280,1280]{1,0:T(8,128)(2,1)S(1)}, bf16[1280,1280]{1,0:T(8,128)(2,1)}, u32[]{:S(2)}) copy-start(bf16[1280,1280]{1,0:T(8,128)(2,1)} %get-tuple-element.46) | copy-start | bytes 9830404
  1329.3 13.6 %copy-start.1 = (f32[3,1280]{1,0:T(4,128)S(1)}, f32[3,1280]{1,0:T(4,128)}, u32[]{:S(2)}) copy-start(f32[3,1280]{1,0:T(4,128)} %param.14) | copy-start | bytes 46084
Sparse Core Ops, SparseCore 0:
  13.1 43.1 all-gather.6
  150.3 51.3 reduce-scatter.4
  206.5 40.4 all-gather.8
  249.0 40.4 all-gather.10
  333.0 51.3 reduce-scatter.8
  386.8 51.3 reduce-scatter.6
  444.7 40.4 all-gather.12
  560.6 51.3 reduce-scatter.10
  617.1 334.5 all-reduce.3
  953.1 376.1 all-gather.14
